TPU v7x, 32 devices: a whole 2x2x4 slice. The times are simulated.
32 devices in a mesh: seq: 16 (over z, x, core), ex: 2 (over y).
Axes of the slice: x: 2, y: 2, z: 4, core: 2. Of those that a mesh axis runs over, the one named last changes fastest.
Arguments:
- acts: bfloat16 [4, 2048, 4096], P('ex', 'seq'), may hold values from -6 to 6
- out_grads: bfloat16 [4, 2048, 5120], P('ex', 'seq'), may hold values from -6 to 6
- lengths: int32 [4], P('ex'), may hold values from 512 to 2048, as said below
- in_tiles: bfloat16 [32, 128, 128], replicated, may hold values from -0.09375 to 0.09375
- in_blocks: int32 [32], replicated, may hold values from 0 to 31, each once
- in_signs: int32 [32, 128], replicated, may hold values 0 or 1
- out_tiles: bfloat16 [40, 128, 64], replicated, may hold values from -0.09375 to 0.09375
- out_blocks: int32 [40], replicated, may hold values from 0 to 39, as said below
- out_signs: int32 [40, 128], replicated, may hold values 0 or 1
- query_grads: bfloat16 [2048, 8192], P('seq', 'ex'), may hold values from -6 to 6
Outputs:
- scores: float32 [4, 2048], P('ex', 'seq')
Inputs may be any that keep to these rules, and one draw needn't show every extreme that they name: `lengths`: every training sequence has at least 512 live positions and some sequence has all 2048. `in_blocks`: a permutation of the 32 input feature blocks. `out_blocks`: the first 32 entries are a permutation of 0 to 31, the last 8 a permutation of 32 to 39.
All inputs are finite; a program needn't handle non-finite values.
Results may differ from a plain program's by a relative error of at most 0.005.
Values may be sent and summed in bfloat16 or wider, within the bound.
A program may use at most 64 MiB of HBM per device.

v0:
```python
import jax
import jax.numpy as jnp
from jax import lax
from jax.sharding import PartitionSpec as P


def place(sketch_tiles, block_ids, sign_bits):
    tile_count = sketch_tiles.shape[0]
    chosen = (block_ids[:, None] == jnp.arange(tile_count, dtype=jnp.int32)[None, :]).astype(
        jnp.float32
    )
    signed = sketch_tiles.astype(jnp.float32) * (2 * sign_bits - 1).astype(jnp.float32)[:, :, None]
    placed = jnp.einsum("bc,bik->cik", chosen, signed, precision=lax.Precision.HIGHEST)
    return placed.reshape(tile_count * sketch_tiles.shape[1], sketch_tiles.shape[2]).astype(
        jnp.bfloat16
    )


def widen(placed, split_at):
    out_cols = placed.shape[1]
    upper = jnp.concatenate([placed[:split_at], jnp.zeros((split_at, out_cols), jnp.bfloat16)], 1)
    lower = jnp.concatenate(
        [jnp.zeros((placed.shape[0] - split_at, out_cols), jnp.bfloat16), placed[split_at:]], 1
    )
    return jnp.concatenate([upper, lower], 0)


def per_device(
    acts,
    out_grads,
    lengths,
    in_tiles,
    in_blocks,
    in_signs,
    out_tiles,
    out_blocks,
    out_signs,
    query_grads,
):
    examples_dev, seq_dev, width = acts.shape
    r_in = place(in_tiles, in_blocks, in_signs)
    r_out = widen(place(out_tiles, out_blocks, out_signs), width)
    offset = lax.axis_index("seq") * seq_dev
    positions = offset + jnp.arange(seq_dev, dtype=jnp.int32)
    live_rows = (positions[None, :] < lengths[:, None]).astype(jnp.float32)
    in_sketched = jnp.dot(
        acts.reshape(examples_dev * seq_dev, width), r_in, preferred_element_type=jnp.float32
    )
    in_sketched = (in_sketched.reshape(examples_dev, seq_dev, -1) * live_rows[:, :, None]).astype(
        jnp.bfloat16
    )
    out_sketched = jnp.dot(
        out_grads.reshape(examples_dev * seq_dev, -1), r_out, preferred_element_type=jnp.float32
    )
    out_sketched = out_sketched.reshape(examples_dev, seq_dev, -1).astype(jnp.bfloat16)
    crossed = jnp.einsum(
        "esa,esc->eac", in_sketched, out_sketched, preferred_element_type=jnp.float32
    )
    in_cols = r_in.shape[1] // 2
    out_cols = r_out.shape[1] // 2
    partial_proj = jnp.stack([crossed[:, :in_cols, :out_cols], crossed[:, in_cols:, out_cols:]], 1)
    partial_proj = partial_proj.reshape(examples_dev, -1) / lengths.astype(jnp.float32)[:, None]
    proj_width = partial_proj.shape[1]
    ex_count = lax.axis_size("ex")
    block_width = proj_width // ex_count
    pieces = partial_proj.reshape(examples_dev, ex_count, block_width)
    moved = lax.all_to_all(pieces, "ex", split_axis=1, concat_axis=0, tiled=True)
    summed = lax.psum(moved, "seq")
    owned = summed.astype(jnp.bfloat16).reshape(examples_dev * ex_count, block_width)
    return lax.psum_scatter(
        lax.dot_general(
            owned, query_grads, (((1,), (1,)), ((), ())), preferred_element_type=jnp.float32
        ),
        "ex",
        scatter_dimension=0,
        tiled=True,
    )


def solution(mesh):
    in_specs = (
        P("ex", "seq", None),
        P("ex", "seq", None),
        P("ex"),
        P(),
        P(),
        P(),
        P(),
        P(),
        P(),
        P("seq", "ex"),
    )
    out_specs = P("ex", "seq")
    return jax.shard_map(
        per_device, mesh=mesh, in_specs=in_specs, out_specs=out_specs, check_vma=False
    )
```

profile of v0, /device:TPU:0, one launch (start us, length us, event | category | flops | bytes accessed | tf_op | source)
XLA Modules:
  0.0 92.1 jit_solution(9811729410962465294)
XLA Ops:
  0.0 0.9 add_convert_fusion
  0.9 1.2 %convert_multiply_fusion.1 = f32[40,128,64]{1,2,0:T(8,128)S(1)} fusion(bf16[40,128,64]{1,2,0:T(8,128)(2,1)} %param.16, f32[40,128]{1,0:T(8,128)S(1)} %add_convert_fusion), kind=kLoop, calls=%fused_computation.15 | loop fusion | flops 655360 | bytes 1986560 | tf_op jit(solution)/shard_map/mul | solution.py:12
  2.1 2.3 %convolution_convert_fusion = bf16[40,128,64]{1,0,2:T(8,128)(2,1)S(1)} fusion(f32[40,128,64]{1,2,0:T(8,128)S(1)} %convert_multiply_fusion.1, s32[40]{0:T(128)} %param.17), kind=kOutput, calls=%fused_computation.8 | convolution fusion | flops 157615680 | bytes 1966240 | tf_op jit(solution)/shard_map/bc,bik->cik/dot_general | solution.py:13
  4.5 0.2 copy.39
  4.8 1.0 %fusion.18 = bf16[256,128]{0,1:T(8,128)(2,1)S(1)} fusion(bf16[256,5120]{1,0:T(8,128)(2,1)S(1)} %bitcast.46, bf16[1024,64]{0,1:T(8,128)(2,1)S(1)} %bitcast.54, bf16[4096,64]{0,1:T(8,128)(2,1)S(1)} %bitcast.50), kind=kOutput, calls=%fused_computation.18 | convolution fusion | flops 340819968 | bytes 3342336 | tf_op jit(solution)/shard_map/dot_general | solution.py:52
  5.8 0.1 copy.25
  5.9 1.8 %convert_multiply_fusion = f32[32,128,128]{2,1,0:T(8,128)S(1)} fusion(bf16[32,128,128]{2,1,0:T(8,128)(2,1)} %param.13, f32[32,128]{1,0:T(8,128)S(1)} %add_convert_fusion.1), kind=kLoop, calls=%fused_computation.6 | loop fusion | flops 1048576 | bytes 3162112 | tf_op jit(solution)/shard_map/mul | solution.py:12
  7.8 2.4 %fusion.4 = bf16[32,128,128]{2,0,1:T(8,128)(2,1)S(1)} fusion(f32[32,128,128]{2,1,0:T(8,128)S(1)} %convert_multiply_fusion, s32[32]{0:T(128)S(1)} %copy-done.3), kind=kOutput, calls=%fused_computation.7 | convolution fusion | flops 201851904 | bytes 3145856 | tf_op jit(solution)/shard_map/bc,bik->cik/dot_general | solution.py:13
  10.2 1.4 %copy.21 = bf16[32,128,128]{2,1,0:T(8,128)(2,1)} copy(bf16[32,128,128]{2,0,1:T(8,128)(2,1)S(1)} %fusion.4) | data formatting | bytes 2097152 | tf_op jit(solution)/shard_map/convert_element_type | solution.py:14
  11.6 0.1 compare_convert_fusion
  11.7 2.7 %convolution_bitcast_fusion = f32[16,2,8,128]{3,2,1,0:T(8,128)S(1)} fusion(bf16[4096,128]{1,0:T(8,128)(2,1)} %bitcast.47, bf16[256,4096]{1,0:T(8,128)(2,1)} %bitcast.48), kind=kOutput, calls=%fused_computation.16 | convolution fusion | flops 268435456 | bytes 3276800 | tf_op jit(solution)/shard_map/dot_general | solution.py:46
  14.4 0.1 fusion.23
  14.6 0.1 fusion.38
  14.7 0.1 stack.10
  14.8 0.1 stack.9
  14.9 0.7 maximum_divide_fusion
  15.6 4.3 %all-to-all-start = ((f32[2,2,4096]{2,0,1:T(2,128)}), f32[2,2,4096]{2,0,1:T(2,128)S(1)}, u32[]{:S(2)}, u32[]{:S(2)}) async-start(f32[2,2,4096]{2,0,1:T(2,128)} %maximum_divide_fusion), calls=%async_computation | async-start | bytes 131072 | tf_op jit(solution)/shard_map/all_to_all | solution.py:67
  19.9 0.6 dynamic-slice
  21.1 2.9 %all-to-all-done = f32[2,2,4096]{2,0,1:T(2,128)S(1)} async-done(((f32[2,2,4096]{2,0,1:T(2,128)}), f32[2,2,4096]{2,0,1:T(2,128)S(1)}, u32[]{:S(2)}, u32[]{:S(2)}) %all-to-all-start) | async-done | bytes 65568 | tf_op jit(solution)/shard_map/all_to_all | solution.py:67
  24.0 0.1 all_to_all.16
  24.0 60.9 %psum.7 = bf16[4,1,4096]{2,0,1:T(4,128)(2,1)S(1)} all-reduce(f32[4,1,4096]{2,0,1:T(4,128)S(1)} %all_to_all.16), channel_id=1, replica_groups=mesh['seq'=16,'ex'=2] {'seq'}, use_global_device_ids=true, to_apply=%region_0.0 | all-reduce | flops 16384 | bytes 98304 | tf_op jit(solution)/shard_map/psum | solution.py:68
  85.0 1.6 %fusion.26 = f32[4,128]{1,0:T(4,128)S(1)} fusion(bf16[128,4096]{1,0:T(8,128)(2,1)} %param.19, bf16[4,1,4096]{2,0,1:T(4,128)(2,1)S(1)} %psum.7), kind=kOutput, calls=%fused_computation.27 | convolution fusion | flops 4194304 | bytes 1083392 | tf_op jit(solution)/shard_map/dot_general | solution.py:71
  86.6 4.9 %all-reduce.2 = f32[4,128]{1,0:T(4,128)S(1)} all-reduce(f32[4,128]{1,0:T(4,128)S(1)} %fusion.26), channel_id=2, replica_groups=mesh['seq'=16,'ex'=2] {'ex'}, use_global_device_ids=true, to_apply=%region_1.0.clone | all-reduce | flops 512 | bytes 4096
  91.5 0.6 constant_dynamic-slice_fusion
  (16 shorter events, 0.1 us)
Async XLA Ops:
  0.0 4.7 %copy-start = (bf16[2,128,5120]{2,1,0:T(8,128)(2,1)S(1)}, bf16[2,128,5120]{2,1,0:T(8,128)(2,1)}, u32[]{:S(2)}) copy-start(bf16[2,128,5120]{2,1,0:T(8,128)(2,1)} %param.11) | copy-start | bytes 7864324
  4.7 1.1 %copy-start.1 = (s32[32,128]{1,0:T(8,128)S(1)}, s32[32,128]{1,0:T(8,128)}, u32[]{:S(2)}) copy-start(s32[32,128]{1,0:T(8,128)} %param.15) | copy-start | bytes 49156
  5.8 2.0 %copy-start.3 = (s32[32]{0:T(128)S(1)}, s32[32]{0:T(128)}, u32[]{:S(2)}) copy-start(s32[32]{0:T(128)} %param.14) | copy-start | bytes 388
  7.8 3.9 %copy-start.2 = (s32[2]{0:T(128)S(1)}, s32[2]{0:T(128)}, u32[]{:S(2)}) copy-start(s32[2]{0:T(128)} %param.12) | copy-start | bytes 28
  11.7 8.2 %copy-start.4 = (u32[32]{0:T(128)S(1)}, u32[32]{0:T(128)}, u32[]{:S(2)}) copy-start(u32[32]{0:T(128)} %constant.25) | copy-start | bytes 388
  15.6 8.4 %all-to-all-start = ((f32[2,2,4096]{2,0,1:T(2,128)}), f32[2,2,4096]{2,0,1:T(2,128)S(1)}, u32[]{:S(2)}, u32[]{:S(2)}) async-start(f32[2,2,4096]{2,0,1:T(2,128)} %maximum_divide_fusion), calls=%async_computation | async-start | bytes 131072 | tf_op jit(solution)/shard_map/all_to_all | solution.py:67
where the time goes:
time: 92.4 us; the launch traced here: 92.1 us
  blocking collectives  65.9 us (71%)
  matrix products  10.2 us (11%)
  other arithmetic  4.75 us (5%)
  starting transfers between devices  4.26 us (5%)
  local copies, waits for them, and re-layouts  3.29 us (4%)
  waiting for transfers between devices  2.89 us (3%)
    psum x1, blocking collectives, per_device(): summed = lax.psum(moved, 'seq')  60.9 us
    unnamed x1, blocking collectives  4.93 us
    dot_general x2, matrix products, place(): jnp.einsum('bc,bik->cik', chosen, signed, precision=lax.Precision.HIGHEST)  4.72 us
    all_to_all x1, starting transfers between devices, per_device(): lax.all_to_all(pieces, 'ex', split_axis=1, concat_axis=0, tiled=True)  4.26 us
    mul x2, other arithmetic, place(): sketch_tiles.astype(jnp.float32)  3.08 us
    all_to_all x1, waiting for transfers between devices, per_device(): lax.all_to_all(pieces, 'ex', split_axis=1, concat_axis=0, tiled=True)  2.89 us
    dot_general x1, matrix products, per_device(): jnp.dot(acts.reshape(examples_dev * seq_dev, width), r_in, preferred_elem...  2.74 us
  transfers between devices with their start and end apart: 1, of which 1 were waited for; matrix products, arithmetic and copies ran while one was open for 1% of the time, Pallas kernels for 0%

commit v1 on v0

--- a/solution.py
+++ b/solution.py
@@ -65,7 +65,7 @@
     block_width = proj_width // ex_count
     pieces = partial_proj.reshape(examples_dev, ex_count, block_width)
     moved = lax.all_to_all(pieces, "ex", split_axis=1, concat_axis=0, tiled=True)
-    summed = lax.psum(moved, "seq")
+    summed = jnp.sum(lax.all_gather(moved, "seq"), axis=0)
     owned = summed.astype(jnp.bfloat16).reshape(examples_dev * ex_count, block_width)
     return lax.psum_scatter(
         lax.dot_general(

time: 92.4 us -> 84.3 us (0.912)
  blocking collectives: 65.9 us -> 13.1 us
  waiting for transfers between devices: 2.89 us -> 37 us
  between operations: 0.82 us -> 14.2 us
  starting transfers between devices: 4.26 us -> 0.01 us
    psum x1 -> x0, blocking collectives: 60.9 us -> none  [per_device(): summed = lax.psum(moved, 'seq')]
    all_gather x0 -> x1, waiting for transfers between devices: none -> 37 us  [per_device(): summed = jnp.sum(lax.all_gather(moved, 'seq'), axis=0)]
    all_to_all x0 -> x1, blocking collectives: none -> 8.19 us  [per_device(): lax.all_to_all(pieces, 'ex', split_axis=1, concat_axis=0, tiled=True)]
    all_to_all x1 -> x0, starting transfers between devices: 4.26 us -> none  [per_device(): lax.all_to_all(pieces, 'ex', split_axis=1, concat_axis=0, tiled=True)]
    all_to_all x1 -> x0, waiting for transfers between devices: 2.89 us -> none  [per_device(): lax.all_to_all(pieces, 'ex', split_axis=1, concat_axis=0, tiled=True)]
    reduce_sum x0 -> x1, other arithmetic: none -> 1.39 us  [per_device(): summed = jnp.sum(lax.all_gather(moved, 'seq'), axis=0)]
where the time goes in v1:
time: 84.3 us; the launch traced here: 84 us
  waiting for transfers between devices  37 us (44%)
  between operations  14.2 us (17%)
  blocking collectives  13.1 us (16%)
  matrix products  10.2 us (12%)
  other arithmetic  5.52 us (7%)
  local copies, waits for them, and re-layouts  3.9 us (5%)
    all_gather x1, waiting for transfers between devices, per_device(): summed = jnp.sum(lax.all_gather(moved, 'seq'), axis=0)  37 us
    all_to_all x1, blocking collectives, per_device(): lax.all_to_all(pieces, 'ex', split_axis=1, concat_axis=0, tiled=True)  8.19 us
    unnamed x1, blocking collectives  4.93 us
    dot_general x2, matrix products, place(): jnp.einsum('bc,bik->cik', chosen, signed, precision=lax.Precision.HIGHEST)  4.72 us
    mul x2, other arithmetic, place(): sketch_tiles.astype(jnp.float32)  3.08 us
    dot_general x1, matrix products, per_device(): jnp.dot(acts.reshape(examples_dev * seq_dev, width), r_in, preferred_elem...  2.75 us
  transfers between devices with their start and end apart: 1, of which 1 were waited for; matrix products, arithmetic and copies ran while one was open for 1% of the time, Pallas kernels for 0%

profile of v1, /device:TPU:0, one launch (start us, length us, event | category | flops | bytes accessed | tf_op | source)
XLA Modules:
  0.0 84.0 jit_solution(12012628926971640523)
XLA Ops:
  6.5 0.9 %add_convert_fusion = f32[40,128]{1,0:T(8,128)S(1)} fusion(s32[40,128]{1,0:T(8,128)} %param.18), kind=kLoop, calls=%fused_computation.29 | loop fusion | flops 15360 | bytes 40960 | tf_op jit(solution)/shard_map/convert_element_type | solution.py:12
  7.4 1.2 %convert_multiply_fusion.1 = f32[40,128,64]{1,2,0:T(8,128)S(1)} fusion(bf16[40,128,64]{1,2,0:T(8,128)(2,1)} %param.16, f32[40,128]{1,0:T(8,128)S(1)} %add_convert_fusion), kind=kLoop, calls=%fused_computation.15 | loop fusion | flops 655360 | bytes 1986560 | tf_op jit(solution)/shard_map/mul | solution.py:12
  8.7 2.3 %convolution_convert_fusion = bf16[40,128,64]{1,0,2:T(8,128)(2,1)S(1)} fusion(f32[40,128,64]{1,2,0:T(8,128)S(1)} %convert_multiply_fusion.1, s32[40]{0:T(128)} %param.17), kind=kOutput, calls=%fused_computation.8 | convolution fusion | flops 157615680 | bytes 1966240 | tf_op jit(solution)/shard_map/bc,bik->cik/dot_general | solution.py:13
  11.0 0.2 copy.39
  11.3 1.0 %fusion.18 = bf16[256,128]{0,1:T(8,128)(2,1)S(1)} fusion(bf16[256,5120]{1,0:T(8,128)(2,1)S(1)} %bitcast.44, bf16[1024,64]{0,1:T(8,128)(2,1)S(1)} %bitcast.52, bf16[4096,64]{0,1:T(8,128)(2,1)S(1)} %bitcast.48), kind=kOutput, calls=%fused_computation.18 | convolution fusion | flops 340819968 | bytes 3342336 | tf_op jit(solution)/shard_map/dot_general | solution.py:52
  12.3 0.1 copy.25
  12.4 1.8 %convert_multiply_fusion = f32[32,128,128]{2,1,0:T(8,128)S(1)} fusion(bf16[32,128,128]{2,1,0:T(8,128)(2,1)} %param.13, f32[32,128]{1,0:T(8,128)S(1)} %add_convert_fusion.1), kind=kLoop, calls=%fused_computation.6 | loop fusion | flops 1048576 | bytes 3162112 | tf_op jit(solution)/shard_map/mul | solution.py:12
  14.3 2.4 %fusion.4 = bf16[32,128,128]{2,0,1:T(8,128)(2,1)S(1)} fusion(f32[32,128,128]{2,1,0:T(8,128)S(1)} %convert_multiply_fusion, s32[32]{0:T(128)S(1)} %copy-done.3), kind=kOutput, calls=%fused_computation.7 | convolution fusion | flops 201851904 | bytes 3145856 | tf_op jit(solution)/shard_map/bc,bik->cik/dot_general | solution.py:13
  16.8 1.4 %copy.21 = bf16[32,128,128]{2,1,0:T(8,128)(2,1)} copy(bf16[32,128,128]{2,0,1:T(8,128)(2,1)S(1)} %fusion.4) | data formatting | bytes 2097152 | tf_op jit(solution)/shard_map/convert_element_type | solution.py:14
  18.1 0.1 compare_convert_fusion
  18.2 2.7 %convolution_bitcast_fusion = f32[16,2,8,128]{3,2,1,0:T(8,128)S(1)} fusion(bf16[4096,128]{1,0:T(8,128)(2,1)} %bitcast.45, bf16[256,4096]{1,0:T(8,128)(2,1)} %bitcast.46), kind=kOutput, calls=%fused_computation.16 | convolution fusion | flops 268435456 | bytes 3276800 | tf_op jit(solution)/shard_map/dot_general | solution.py:46
  21.0 0.1 fusion.23
  21.1 0.1 fusion.37
  21.2 0.1 stack.10
  21.3 0.1 stack.9
  21.4 0.1 maximum_divide_fusion
  21.5 8.2 %all_to_all.15 = f32[2,2,4096]{2,0,1:T(2,128)S(1)} all-to-all(f32[2,2,4096]{2,0,1:T(2,128)S(1)} %maximum_divide_fusion), channel_id=1, replica_groups=mesh['seq'=16,'ex'=2] {'ex'}, dimensions={1} | all-to-all | bytes 131072 | tf_op jit(solution)/shard_map/all_to_all | solution.py:67
  29.7 0.7 all_gather.6
  30.4 0.6 dynamic-slice
  31.7 37.0 %all-gather.2.cloned.1.call-done = f32[16,4,1,4096]{3,1,2,0:T(4,128)} async-done(((f32[1,4,1,4096]{3,1,2,0:T(4,128)}), f32[16,4,1,4096]{3,1,2,0:T(4,128)}) %all-gather.2.cloned.1.call-update) | async-done | bytes 1048592 | tf_op jit(solution)/shard_map/all_gather | solution.py:68
  68.7 1.4 %reduce_sum.9 = bf16[4,4096]{1,0:T(4,128)(2,1)S(1)} reduce(f32[16,4,1,4096]{3,1,2,0:T(4,128)} %all-gather.2.cloned.1.call-done, f32[]{:T(128)} %constant.20.clone.1), dimensions={0,2}, to_apply=%region_0.0 | reduce | flops 245760 | bytes 1081348 | tf_op jit(solution)/shard_map/reduce_sum | solution.py:68
  70.1 1.6 %fusion.38 = f32[4,128]{1,0:T(4,128)S(1)} fusion(bf16[4,4096]{1,0:T(4,128)(2,1)S(1)} %reduce_sum.9, bf16[128,4096]{1,0:T(8,128)(2,1)} %param.19), kind=kOutput, calls=%fused_computation.44 | convolution fusion | flops 4194304 | bytes 1083392 | tf_op jit(solution)/shard_map/dot_general | solution.py:71
  71.7 4.9 %all-reduce.2 = f32[4,128]{1,0:T(4,128)S(1)} all-reduce(f32[4,128]{1,0:T(4,128)S(1)} %fusion.38), channel_id=2, replica_groups=mesh['seq'=16,'ex'=2] {'ex'}, use_global_device_ids=true, to_apply=%region_1.0.clone | all-reduce | flops 512 | bytes 4096
  76.6 0.6 constant_dynamic-slice_fusion
  (18 shorter events, 0.1 us)
Async XLA Ops:
  6.5 4.7 %copy-start = (bf16[2,128,5120]{2,1,0:T(8,128)(2,1)S(1)}, bf16[2,128,5120]{2,1,0:T(8,128)(2,1)}, u32[]{:S(2)}) copy-start(bf16[2,128,5120]{2,1,0:T(8,128)(2,1)} %param.11) | copy-start | bytes 7864324
  6.5 62.1 %all-gather.2.cloned.1.call-start = ((), (), s32[]{:S(2)}) async-start(), calls=%async_computation.1 | async-start | bytes 1114112 | tf_op jit(solution)/shard_map/all_gather | solution.py:68
  11.3 1.1 %copy-start.1 = (s32[32,128]{1,0:T(8,128)S(1)}, s32[32,128]{1,0:T(8,128)}, u32[]{:S(2)}) copy-start(s32[32,128]{1,0:T(8,128)} %param.15) | copy-start | bytes 49156
  12.3 2.0 %copy-start.3 = (s32[32]{0:T(128)S(1)}, s32[32]{0:T(128)}, u32[]{:S(2)}) copy-start(s32[32]{0:T(128)} %param.14) | copy-start | bytes 388
  14.3 3.8 %copy-start.2 = (s32[2]{0:T(128)S(1)}, s32[2]{0:T(128)}, u32[]{:S(2)}) copy-start(s32[2]{0:T(128)} %param.12) | copy-start | bytes 28
  18.2 12.2 %copy-start.4 = (u32[32]{0:T(128)S(1)}, u32[32]{0:T(128)}, u32[]{:S(2)}) copy-start(u32[32]{0:T(128)} %constant.27) | copy-start | bytes 388
Sparse Core Ops, SparseCore 0:
  30.5 38.1 all-gather.1
